TPU v7x, 32 devices: a whole 2x2x4 slice. The times are simulated.
32 devices in a mesh: gx: 4 (over x, core), gy: 8 (over z, y).
Axes of the slice: x: 2, y: 2, z: 4, core: 2. Of those that a mesh axis runs over, the one named last changes fastest.
Arguments:
- snapshots: bfloat16 [2, 8192, 8192], P(None, 'gx', 'gy'), may hold values from -200 to 200
- mode_one_test: bfloat16 [2, 8192, 128], P(None, 'gy'), may hold values from -0.148231765 to 0.148231765
- mode_two_test: bfloat16 [2, 8192, 128], P(None, 'gx'), may hold values from -0.046875 to 0.046875
- row_sketch: bfloat16 [256, 8192], P(None, 'gx'), may hold values from -0.0625 to 0.0625
- column_sketch: bfloat16 [256, 8192], P(None, 'gy'), may hold values from -0.0625 to 0.0625
- old_mode_one: float32 [8192, 128], P('gx'), may hold values from -3 to 3
- old_mode_two: float32 [8192, 128], P('gy'), may hold values from -3 to 3
- old_core: float32 [9, 256, 256], replicated, may hold values from -3 to 3
- time_mix: float32 [9, 2], replicated, may hold values from -2.5 to 2.5
Outputs:
- basis: float32 [8192, 128], P(('gx', 'gy'))
- mode_two: float32 [8192, 128], P('gy')
- projected: float32 [128, 2, 8192], P('gx', None, 'gy')
- core: float32 [9, 256, 256], replicated
All inputs are finite; a program needn't handle non-finite values.
Results may differ from a plain program's by a relative error of at most 0.0024.
Values may be sent and summed in bfloat16 or wider, within the bound.
No kernel may reach another device: no remote copies, remote signals or barrier semaphores. Data moves between devices by JAX's collectives and lax.ppermute only.
A program may use at most 128 MiB of HBM per device.

v0:
```python
import math

import jax
import jax.numpy as jnp
from jax import lax
from jax.sharding import PartitionSpec as P


def orthonormal(sketch_rows, gram_matrix, root_rows):
    factor = jnp.linalg.cholesky(gram_matrix)
    return root_rows * jax.scipy.linalg.solve_triangular(factor, sketch_rows.T, lower=True).T


def body(
    snapshots,
    mode_one_test,
    mode_two_test,
    row_sketch,
    column_sketch,
    old_mode_one,
    old_mode_two,
    old_core,
    time_mix,
):
    tile_rows = snapshots.shape[1]
    root_rows = math.sqrt(tile_rows * lax.axis_size("gx"))
    part_two = jnp.einsum(
        "trc,trk->ck", snapshots, mode_two_test, preferred_element_type=jnp.float32
    )
    mode_two = old_mode_two + lax.psum(part_two, "gx")
    part_one = jnp.einsum(
        "trc,tck->rk", snapshots, mode_one_test, preferred_element_type=jnp.float32
    )
    folded = jnp.einsum("sr,trc->tsc", row_sketch, snapshots, preferred_element_type=jnp.float32)
    core_part = jnp.einsum(
        "tsc,uc->tsu", folded, column_sketch.astype(jnp.float32), precision=lax.Precision.HIGHEST
    )
    core_part = jnp.einsum("jt,tsu->jsu", time_mix, core_part, precision=lax.Precision.HIGHEST)
    core = old_core + lax.psum(core_part, ("gx", "gy"))
    row_share = tile_rows // lax.axis_size("gy")
    first_row = lax.axis_index("gy") * row_share
    whole_rows = lax.psum(part_one, "gy") + old_mode_one
    gram_matrix = lax.psum(jnp.dot(whole_rows.T, whole_rows, precision=lax.Precision.HIGHEST), "gx")
    full_basis = orthonormal(whole_rows, gram_matrix, root_rows)
    projected_part = jnp.einsum(
        "rk,trc->ktc",
        full_basis.astype(jnp.bfloat16),
        snapshots,
        preferred_element_type=jnp.float32,
    )
    basis_out = lax.dynamic_slice_in_dim(full_basis, first_row, row_share, 0)
    projected = lax.psum_scatter(projected_part, "gx", scatter_dimension=0, tiled=True) / root_rows
    return (basis_out, mode_two, projected, core)


def solution(mesh):
    placed = (
        P(None, "gx", "gy"),
        P(None, "gy", None),
        P(None, "gx", None),
        P(None, "gx"),
        P(None, "gy"),
        P("gx", None),
        P("gy", None),
        P(),
        P(),
    )
    return jax.shard_map(
        body,
        mesh=mesh,
        in_specs=placed,
        out_specs=(P(("gx", "gy"), None), P("gy", None), P("gx", None, "gy"), P()),
        check_vma=False,
    )
```

profile of v0, /device:TPU:0, one launch (start us, length us, event | category | flops | bytes accessed | tf_op | source)
XLA Modules:
  0.0 316.1 jit_solution(14542344356930116117)
XLA Ops:
  7.2 6.8 %convolution_bitcast_fusion = f32[2048,128]{1,0:T(8,128)} fusion(bf16[2,2048,1024]{2,1,0:T(8,128)(2,1)} %param.9, bf16[2,1024,128]{2,1,0:T(8,128)(2,1)} %param.10), kind=kOutput, calls=%fused_computation.1 | convolution fusion | flops 1073741824 | bytes 9961472 | tf_op jit(solution)/shard_map/trc,tck->rk/dot_general | solution.py:31
  14.2 6.1 %fusion.2 = f32[2,1024,256]{2,1,0:T(8,128)S(1)} fusion(bf16[2,2048,1024]{2,1,0:T(8,128)(2,1)} %param.9, bf16[256,2048]{1,0:T(8,128)(2,1)S(1)} %copy-done), kind=kOutput, calls=%fused_computation.7 | convolution fusion | flops 2147483648 | bytes 11534336 | tf_op jit(solution)/shard_map/sr,trc->tsc/dot_general | solution.py:34
  20.3 1.8 fusion
  22.2 6.6 %convolution_bitcast_fusion.2 = f32[1024,128]{1,0:T(8,128)} fusion(bf16[2,2048,1024]{2,1,0:T(8,128)(2,1)} %param.9, bf16[2,2048,128]{2,1,0:T(8,128)(2,1)S(1)} %copy-done.5), kind=kOutput, calls=%fused_computation.6 | convolution fusion | flops 1073741824 | bytes 9961472 | tf_op jit(solution)/shard_map/trc,trk->ck/dot_general | solution.py:27
  28.7 66.5 %all-reduce.5.cloned.1.call-done = f32[2048,128]{1,0:T(8,128)} async-done(((f32[2048,128]{1,0:T(8,128)}), f32[2048,128]{1,0:T(8,128)}) %all-reduce.5.cloned.1.call-update) | async-done | bytes 1048592 | tf_op jit(solution)/shard_map/psum | solution.py:42
  95.3 1.6 add.34
  96.9 2.4 fusion.13
  99.5 5.1 %convolution_bitcast_fusion.1 = f32[9,256,256]{2,0,1:T(8,128)} fusion(f32[2,256,256]{2,1,0:T(8,128)S(1)} %fusion, f32[9,2]{0,1:T(2,128)S(1)} %copy-done.4), kind=kOutput, calls=%fused_computation.3 | convolution fusion | flops 14155776 | bytes 2883656 | tf_op jit(solution)/shard_map/jt,tsu->jsu/dot_general | solution.py:38
  104.8 28.2 %all-reduce.9.cloned.1.call-done = (f32[128,128]{0,1:T(8,128)}, f32[1024,128]{1,0:T(8,128)}) async-done(((f32[128,128]{0,1:T(8,128)}, f32[1024,128]{1,0:T(8,128)}), (f32[128,128]{0,1:T(8,128)}, f32[1024,128]{1,0:T(8,128)})) %all-reduce.9.cloned.1.call-update) | async-done | bytes 589840 | tf_op jit(solution)/shard_map/psum | solution.py:43
  133.0 0.9 copy.14
  133.9 0.9 fusion.11
  134.8 11.7 %cholesky.16 = f32[128,128]{1,0:T(8,128)S(1)} custom-call(f32[128,128]{1,0:T(8,128)S(1)} %fusion.11), custom_call_target="Cholesky" | custom-call | tf_op jit(solution)/shard_map/jit(cholesky)/cholesky | solution.py:10
  147.2 0.7 fusion.9
  147.8 9.8 %custom-call.7 = f32[1,128,128]{1,2,0:T(8,128)S(1)} custom-call(f32[1,128,128]{2,1,0:T(8,128)S(1)} %fusion.9), custom_call_target="InvertDiagBlocksLowerTriangular" | custom-call | tf_op jit(solution)/shard_map/jit(_solve_triangular)/triangular_solve | solution.py:11
  157.7 1.0 convolution_multiply_fusion
  158.6 5.8 %fusion.5 = f32[128,2,1024]{2,0,1:T(8,128)} fusion(bf16[2,2048,1024]{2,1,0:T(8,128)(2,1)} %param.9, f32[2048,128]{1,0:T(8,128)S(1)} %convolution_multiply_fusion), kind=kOutput, calls=%fused_computation.10 | convolution fusion | flops 1074003968 | bytes 10485760 | tf_op jit(solution)/shard_map/rk,trc->ktc/dot_general | solution.py:45
  164.4 116.8 %all-reduce.7.cloned.1.call-done = f32[9,256,256]{2,0,1:T(8,128)} async-done(((f32[9,256,256]{2,0,1:T(8,128)}), f32[9,256,256]{2,0,1:T(8,128)}) %all-reduce.7.cloned.1.call-update) | async-done | bytes 2359312 | tf_op jit(solution)/shard_map/psum | solution.py:39
  281.3 4.6 %copy_add_fusion = f32[9,256,256]{2,0,1:T(8,128)S(1)} fusion(f32[9,256,256]{2,0,1:T(8,128)} %all-reduce.7.cloned.1.call-done, f32[9,256,256]{2,1,0:T(8,128)} %param.16), kind=kLoop, calls=%fused_computation | loop fusion | flops 589824 | bytes 7077888 | tf_op jit(solution)/shard_map/add | solution.py:39
  285.8 2.8 copy.19
  288.6 0.8 add.37
  289.5 0.7 constant_dynamic-slice_fusion
  290.1 17.5 %reduce-scatter.2.cloned.1.call-done = f32[32,2,1024]{2,0,1:T(8,128)} async-done(((f32[128,2,1024]{2,0,1:T(8,128)}), f32[32,2,1024]{2,0,1:T(8,128)}) %reduce-scatter.2.cloned.1.call-update) | async-done | bytes 262160 | tf_op jit(solution)/shard_map/reduce_scatter | solution.py:52
  307.7 1.0 broadcast_multiply_fusion
  308.7 0.9 copy.18
  (22 shorter events, 1.1 us)
Async XLA Ops:
  7.2 7.0 %copy-start = (bf16[256,2048]{1,0:T(8,128)(2,1)S(1)}, bf16[256,2048]{1,0:T(8,128)(2,1)}, u32[]{:S(2)}) copy-start(bf16[256,2048]{1,0:T(8,128)(2,1)} %param.12) | copy-start | bytes 3145732
  7.2 88.1 %all-reduce.5.cloned.1.call-start = ((), (), s32[]{:S(2)}) async-start(), calls=%async_computation.1 | async-start | bytes 2097152 | tf_op jit(solution)/shard_map/psum | solution.py:42
  14.1 6.2 %copy-start.3 = (bf16[256,1024]{1,0:T(8,128)(2,1)S(1)}, bf16[256,1024]{1,0:T(8,128)(2,1)}, u32[]{:S(2)}) copy-start(bf16[256,1024]{1,0:T(8,128)(2,1)} %param.13) | copy-start | bytes 1572868
  14.1 118.9 %all-reduce.9.cloned.1.call-start = ((), (), s32[]{:S(2)}) async-start(), calls=%async_computation.4 | async-start | bytes 1179648 | tf_op jit(solution)/shard_map/psum | solution.py:43
  14.1 8.0 %copy-start.5 = (bf16[2,2048,128]{2,1,0:T(8,128)(2,1)S(1)}, bf16[2,2048,128]{2,1,0:T(8,128)(2,1)}, u32[]{:S(2)}) copy-start(bf16[2,2048,128]{2,1,0:T(8,128)(2,1)} %param.11) | copy-start | bytes 3145732
  28.7 70.7 %copy-start.4 = (f32[9,2]{0,1:T(2,128)S(1)}, f32[9,2]{0,1:T(2,128)}, u32[]{:S(2)}) copy-start(f32[9,2]{0,1:T(2,128)} %param.17) | copy-start | bytes 220
  99.4 181.9 %all-reduce.7.cloned.1.call-start = ((), (), s32[]{:S(2)}) async-start(), calls=%async_computation.3 | async-start | bytes 8388608 | tf_op jit(solution)/shard_map/psum | solution.py:39
  104.6 203.1 %reduce-scatter.2.cloned.1.call-start = ((), (), s32[]{:S(2)}) async-start(), calls=%async_computation.2 | async-start | bytes 1310720 | tf_op jit(solution)/shard_map/reduce_scatter | solution.py:52
  285.8 2.8 copy-start.1
  285.8 2.8 copy-start.2
Sparse Core Ops, SparseCore 0:
  14.2 81.0 all-reduce.4
  99.5 33.4 all-reduce.8
  138.5 142.6 all-reduce.6
  283.6 23.9 reduce-scatter.1
where the time goes:
time: 316 us
  waiting for transfers between devices  229 us (72%)
  matrix products  35.6 us (11%)
  other arithmetic  31.7 us (10%)
  between operations  13.9 us (4%)
  local copies, waits for them, and re-layouts  5.31 us (2%)
    psum x1, waiting for transfers between devices, body(): core = old_core + lax.psum(core_part, ('gx', 'gy'))  117 us
    psum x1, waiting for transfers between devices, body(): whole_rows = lax.psum(part_one, 'gy') + old_mode_one  66.5 us
    psum x1, waiting for transfers between devices, body(): lax.psum(jnp.dot(whole_rows.T, whole_rows, precision=lax.Precision.HIGHES...  28.2 us
    reduce_scatter x1, waiting for transfers between devices, body(): lax.psum_scatter(projected_part, 'gx', scatter_dimension=0, tiled=True)  17.5 us
    another operation x3, other arithmetic, orthonormal(): factor = jnp.linalg.cholesky(gram_matrix)  12.4 us
    another operation x2, other arithmetic, orthonormal(): jax.scipy.linalg.solve_triangular(factor, sketch_rows.T, lower=True)  10.5 us
    dot_general x1, matrix products, body(): jnp.einsum('trc,tck->rk', snapshots, mode_one_test, preferred_element_typ...  6.82 us
    dot_general x1, matrix products, body(): jnp.einsum('trc,trk->ck', snapshots, mode_two_test, preferred_element_typ...  6.59 us
  transfers between devices with their start and end apart: 4, of which 4 were waited for; matrix products, arithmetic and copies ran while one was open for 19% of the time, Pallas kernels for 0%

commit v1 on v0

v1 whole, which is shorter than its diff:
```python
import functools
import math

import jax
import jax.numpy as jnp
from jax import lax
from jax.experimental import pallas as pl
from jax.experimental.pallas import tpu as pltpu
from jax.sharding import PartitionSpec as P


HIGHEST = lax.Precision.HIGHEST
F32 = jnp.float32
BF16 = jnp.bfloat16


MIB = 1 << 20
WIDE_LIMIT = 58 * MIB


def exchange(value, axis, bit):
    size = lax.axis_size(axis)
    return lax.ppermute(value, axis, [(i, i ^ bit) for i in range(size)])


def halves(value, bit, axis):
    size = value.shape[0] // 2
    upper = (lax.axis_index(axis) & bit) // bit
    keep = lax.dynamic_slice_in_dim(value, upper * size, size, 0)
    send = lax.dynamic_slice_in_dim(value, (1 - upper) * size, size, 0)
    return keep, send


def joined(mine, other, bit, axis):
    upper = (lax.axis_index(axis) & bit) != 0
    return jnp.where(upper, jnp.concatenate([other, mine]), jnp.concatenate([mine, other]))


def bits_of(size):
    return [1 << i for i in range(size.bit_length() - 1)]


HBM = pl.BlockSpec(memory_space=pltpu.HBM)
VMEM = pl.BlockSpec(memory_space=pltpu.VMEM)


def split(value):
    high = value.astype(BF16)
    return high, (value - high.astype(F32)).astype(BF16)


def mode_one_kernel(groups, snap_hbm, test_hbm, *refs):
    outs = refs[: len(groups)]
    snap, test, snap_sem, test_sem = refs[len(groups) :]
    along = lax.axis_index("gy")
    moments, block = snap.shape[1:3]
    rank = outs[0].shape[2]
    lanes = [slice(t * rank, (t + 1) * rank) for t in range(moments)]
    test_copies = [
        pltpu.make_async_copy(test_hbm.at[t], test.at[:, lanes[t]], test_sem.at[t])
        for t in range(moments)
    ]
    copies = []
    for index, name in enumerate(name for group in groups for name in group):
        start = pl.multiple_of((along ^ name) * block, block)
        copies.append(
            pltpu.make_async_copy(
                snap_hbm.at[:, pl.ds(start, block), :], snap.at[index], snap_sem.at[index]
            )
        )
    for copy in test_copies + copies:
        copy.start()
    for copy in test_copies:
        copy.wait()
    index = 0
    for group, out in zip(groups, outs):
        for i in range(len(group)):
            copies[index].wait()
            both = [
                jnp.dot(snap[index, t], test[...], preferred_element_type=F32)
                for t in range(moments)
            ]
            total = both[0][:, lanes[0]]
            for t in range(1, moments):
                total += both[t][:, lanes[t]]
            out[i] = total
            index += 1


def mode_one_blocks(groups, snapshots, test, block):
    moments, _, cols = snapshots.shape
    rank = test.shape[2]
    count = sum(len(group) for group in groups)
    return pl.pallas_call(
        functools.partial(mode_one_kernel, groups),
        in_specs=[HBM, HBM],
        out_specs=[VMEM] * len(groups),
        out_shape=[jax.ShapeDtypeStruct((len(group), block, rank), F32) for group in groups],
        scratch_shapes=[
            pltpu.VMEM((count, moments, block, cols), snapshots.dtype),
            pltpu.VMEM((cols, moments * rank), test.dtype),
            pltpu.SemaphoreType.DMA((count,)),
            pltpu.SemaphoreType.DMA((moments,)),
        ],
        cost_estimate=pl.CostEstimate(
            flops=4 * moments * count * block * cols * rank,
            bytes_accessed=4 * moments * count * block * cols,
            transcendentals=0,
        ),
        compiler_params=pltpu.CompilerParams(vmem_limit_bytes=WIDE_LIMIT),
        name="mode_one",
    )(snapshots, test)


def load_snapshots(order, snap_hbm, snap, sems):
    rows = snap.shape[1]
    pieces = sems.shape[1]
    block = rows // pieces
    copies = {}
    for n, t in enumerate(order):
        for i in range(pieces):
            span = pl.ds(i * block, block)
            copies[n, i] = pltpu.make_async_copy(
                snap_hbm.at[t, span, :], snap.at[n, span, :], sems.at[n, i]
            )
            copies[n, i].start()
    return copies, block


def core_kernel(snap_hbm, row_ref, column_ref, sent_ref, kept_ref, snap, total, sems):
    rank = kept_ref.shape[2]
    upper = lax.axis_index("gx") & 1
    copies, block = load_snapshots((1 - upper, upper), snap_hbm, snap, sems)
    contract = (((1,), (1,)), ((), ()))
    for n, out_ref in enumerate((sent_ref, kept_ref)):
        for i in range(sems.shape[1]):
            copies[n, i].wait()
            span = slice(i * block, (i + 1) * block)
            term = jnp.dot(row_ref[:, span], snap[n, span, :], preferred_element_type=F32)
            if i == 0:
                total[...] = term
            else:
                total[...] += term
        high, low = split(total[...])
        for g in range(out_ref.shape[0]):
            columns = column_ref[g * rank : (g + 1) * rank, :]
            out_ref[g] = lax.dot_general(
                high, columns, contract, preferred_element_type=F32
            ) + lax.dot_general(low, columns, contract, preferred_element_type=F32)


def core_products(snapshots, row_sketch, column_sketch, rank):
    moments, rows, cols = snapshots.shape
    sketch = row_sketch.shape[0]
    half = jax.ShapeDtypeStruct((sketch // rank, sketch, rank), F32)
    return pl.pallas_call(
        core_kernel,
        in_specs=[HBM, VMEM, VMEM],
        out_specs=[VMEM, VMEM],
        out_shape=[half, half],
        scratch_shapes=[
            pltpu.VMEM((moments, rows, cols), snapshots.dtype),
            pltpu.VMEM((sketch, cols), F32),
            pltpu.SemaphoreType.DMA((moments, 2)),
        ],
        cost_estimate=pl.CostEstimate(
            flops=4 * moments * rows * cols * sketch,
            bytes_accessed=2 * moments * rows * cols,
            transcendentals=0,
        ),
        compiler_params=pltpu.CompilerParams(vmem_limit_bytes=WIDE_LIMIT),
        name="core_tile",
    )(snapshots, row_sketch, column_sketch)


def two_kernel(snap_hbm, test_ref, sent_ref, kept_ref, snap, factors, total, turned, sems):
    moments = snap.shape[0]
    size = kept_ref.shape[0]
    upper = lax.axis_index("gx") & 1
    copies, block = load_snapshots(range(moments), snap_hbm, snap, sems)
    for t in range(moments):
        factors[t] = test_ref[t].T
    for t in range(moments):
        for i in range(sems.shape[1]):
            copies[t, i].wait()
            span = slice(i * block, (i + 1) * block)
            term = jnp.dot(factors[t, :, span], snap[t, span, :], preferred_element_type=F32)
            if t == 0 and i == 0:
                total[...] = term
            else:
                total[...] += term
    turned[...] = total[...].T
    kept_ref[...] = turned[pl.ds(pl.multiple_of(upper * size, size), size), :]
    sent_ref[...] = turned[pl.ds(pl.multiple_of((1 - upper) * size, size), size), :]


def two_products(snapshots, two_test):
    moments, rows, cols = snapshots.shape
    rank = two_test.shape[2]
    half = jax.ShapeDtypeStruct((cols // 2, rank), F32)
    return pl.pallas_call(
        two_kernel,
        in_specs=[HBM, VMEM],
        out_specs=[VMEM, VMEM],
        out_shape=[half, half],
        scratch_shapes=[
            pltpu.VMEM((moments, rows, cols), snapshots.dtype),
            pltpu.VMEM((moments, rank, rows), BF16),
            pltpu.VMEM((rank, cols), F32),
            pltpu.VMEM((cols, rank), F32),
            pltpu.SemaphoreType.DMA((moments, 2)),
        ],
        cost_estimate=pl.CostEstimate(
            flops=4 * moments * rows * cols * rank,
            bytes_accessed=2 * moments * rows * cols,
            transcendentals=0,
        ),
        compiler_params=pltpu.CompilerParams(vmem_limit_bytes=WIDE_LIMIT),
        name="two_tile",
    )(snapshots, two_test)


def gram_kernel(
    names, mine_ref, other_ref, core_ref, core_moved_ref, old_hbm, rows_ref, gram_ref, old, sem
):
    along = lax.axis_index("gy")
    count, block, rank = mine_ref.shape
    copies = []
    for i, name in enumerate(names):
        start = pl.multiple_of((along ^ name) * block, block)
        copies.append(
            pltpu.make_async_copy(old_hbm.at[pl.ds(start, block), :], old.at[i], sem.at[i])
        )
    for copy in copies:
        copy.start()
    gram = jnp.zeros((rank, rank), F32)
    for i in range(count):
        copies[i].wait()
        value = mine_ref[i] + other_ref[count - 1 - i] + old[i]
        rows_ref[i * block : (i + 1) * block, :] = value
        gram += lax.dot_general(
            value, value, (((0,), (0,)), ((), ())), precision=HIGHEST, preferred_element_type=F32
        )
    gram_ref[...] = gram
    rows_ref[count * block :, :] = core_ref[...] + core_moved_ref[...]


def finish_rows(names, mine, other, core_block, core_moved, old):
    count, block, rank = mine.shape
    return pl.pallas_call(
        functools.partial(gram_kernel, names),
        in_specs=[VMEM] * 4 + [HBM],
        out_specs=[VMEM, VMEM],
        out_shape=[
            jax.ShapeDtypeStruct((count * block + core_block.shape[0], rank), F32),
            jax.ShapeDtypeStruct((rank, rank), F32),
        ],
        scratch_shapes=[pltpu.VMEM((count, block, rank), F32), pltpu.SemaphoreType.DMA((count,))],
        compiler_params=pltpu.CompilerParams(vmem_limit_bytes=8 * MIB),
        name="gram",
    )(mine, other, core_block, core_moved, old)


def invert_factor(gram, inverse_ref):
    size = gram.shape[0]
    groups = size // 8
    left = [gram[8 * q : 8 * q + 8, :] for q in range(groups)]
    row = lax.broadcasted_iota(jnp.int32, (8, size), 0)
    column = lax.broadcasted_iota(jnp.int32, (8, size), 1)
    right = [jnp.where(column == row + 8 * q, 1.0, 0.0).astype(F32) for q in range(groups)]

    def spread(value, i):
        return jnp.broadcast_to(value[i : i + 1, :], (8, size))

    def column_of(value, c):
        return jnp.broadcast_to(value[:, c : c + 1], (8, size))

    for p in range(groups):
        panel = [column_of(left[p], 8 * p + k) for k in range(8)]
        pivots = jnp.ones((8, size), F32)
        inverses = []
        for j in range(8):
            pivot = spread(panel[j], j)
            pivots = jnp.where(row == j, pivot, pivots)
            inverses.append(1.0 / pivot)
            factor = jnp.where(row > j, panel[j] * inverses[j], 0.0)
            for k in range(j + 1, 8):
                panel[k] = panel[k] - factor * spread(panel[k], j)
            left[p] = left[p] - factor * spread(left[p], j)
            right[p] = right[p] - factor * spread(right[p], j)
        inverse_ref[8 * p : 8 * p + 8, :] = right[p] * lax.rsqrt(pivots)
        upper = {(k, j): spread(panel[k], j) for j in range(8) for k in range(j + 1, 8)}
        left_rows = [spread(left[p], j) for j in range(8)]
        right_rows = [spread(right[p], j) for j in range(8)]
        for q in range(p + 1, groups):
            below = [column_of(left[q], 8 * p + k) for k in range(8)]
            for j in range(8):
                factor = below[j] * inverses[j]
                for k in range(j + 1, 8):
                    below[k] = below[k] - factor * upper[k, j]
                left[q] = left[q] - factor * left_rows[j]
                right[q] = right[q] - factor * right_rows[j]


def product(a, b):
    contract = (((1,), (1,)), ((), ()))
    (a_high, a_low), (b_high, b_low) = split(a), split(b)
    total = lax.dot_general(a_high, b_low, contract, preferred_element_type=F32)
    total += lax.dot_general(a_low, b_high, contract, preferred_element_type=F32)
    return total + lax.dot_general(a_high, b_high, contract, preferred_element_type=F32)


def finish_kernel(root_rows, names, places, sizes, gram_ref, moved_ref, snap_hbm, *refs):
    parts = len(sizes)
    pieces = refs[:parts]
    own_ref = refs[parts]
    inverse, turned, low, total, snap, sems = refs[-6:]
    outs = refs[parts + 1 : -6]
    along, across = lax.axis_index("gy"), lax.axis_index("gx")
    moments, count, block, _ = snap.shape
    copies = {}
    for t in range(moments):
        for i, name in enumerate(names):
            start = pl.multiple_of((along ^ name) * block, block)
            copies[t, i] = pltpu.make_async_copy(
                snap_hbm.at[t, pl.ds(start, block), :], snap.at[t, i], sems.at[t, i]
            )
            copies[t, i].start()
    invert_factor(gram_ref[...] + moved_ref[...], inverse)
    share = inverse.shape[0] // len(places)
    for k, place in enumerate(places):
        start = pl.multiple_of((across ^ place) * share, share)
        turned[k * share : (k + 1) * share, :] = inverse[pl.ds(start, share), :]
    at = 0
    for piece, size in zip(pieces, sizes):
        low[:, at : at + size] = (root_rows * product(turned[...], piece[:size, :])).astype(BF16)
        at += size
    for t in range(moments):
        for i in range(count):
            copies[t, i].wait()
            term = jnp.dot(
                low[:, i * block : (i + 1) * block], snap[t, i], preferred_element_type=F32
            )
            if i == 0:
                total[...] = term
            else:
                total[...] += term
        sent_ref, passed_ref, kept_ref = outs[3 * t : 3 * t + 3]
        shares = len(places) // 2
        kept_ref[...] = total[:share, :]
        for k in range(1, shares):
            passed_ref[k - 1] = total[k * share : (k + 1) * share, :]
        for k in range(shares):
            sent_ref[k] = total[(shares + k) * share : (shares + k + 1) * share, :]
    own_ref[...] = root_rows * product(pieces[0][:block, :], inverse[...])


def finish(names, places, gram, moved, snapshots, pieces, sizes, root_rows):
    rank = gram.shape[0]
    moments, rows, cols = snapshots.shape
    block = rows // len(names)
    share = rank // len(places)
    half = len(places) // 2
    shapes = [jax.ShapeDtypeStruct((block, rank), F32)]
    for _ in range(moments):
        shapes += [
            jax.ShapeDtypeStruct((half, share, cols), F32),
            jax.ShapeDtypeStruct((half - 1, share, cols), F32),
            jax.ShapeDtypeStruct((share, cols), F32),
        ]
    return pl.pallas_call(
        functools.partial(finish_kernel, root_rows, names, places, sizes),
        in_specs=[VMEM, VMEM, HBM] + [VMEM] * len(pieces),
        out_specs=[VMEM] * len(shapes),
        out_shape=shapes,
        scratch_shapes=[
            pltpu.VMEM((rank, rank), F32),
            pltpu.VMEM((rank, rank), F32),
            pltpu.VMEM((rank, rows), BF16),
            pltpu.VMEM((rank, cols), F32),
            pltpu.VMEM((moments, len(names), block, cols), snapshots.dtype),
            pltpu.SemaphoreType.DMA((moments, len(names))),
        ],
        cost_estimate=pl.CostEstimate(
            flops=8 * rows * cols * rank, bytes_accessed=4 * rows * cols, transcendentals=0
        ),
        compiler_params=pltpu.CompilerParams(vmem_limit_bytes=WIDE_LIMIT),
        name="finish",
    )(gram, moved, snapshots, *pieces)


def body(
    snapshots,
    mode_one_test,
    mode_two_test,
    row_sketch,
    column_sketch,
    old_mode_one,
    old_mode_two,
    old_core,
    time_mix,
):
    moments, tile_rows, _ = snapshots.shape
    rank = mode_one_test.shape[2]
    wide, deep = lax.axis_size("gx"), lax.axis_size("gy")
    bits_x, bits_y = bits_of(wide), bits_of(deep)
    root_rows = math.sqrt(tile_rows * wide)
    block = tile_rows // deep

    scatter_bits, last = bits_y[:-1], bits_y[-1]
    first, rest = scatter_bits[0], scatter_bits[1:]

    names = range(deep)
    early = [j for j in names if j & first and j & rest[0]]
    late = [j for j in names if j & first and not j & rest[0]]
    high_names = [j ^ first for j in early]
    low_names = [j ^ first for j in late]
    (early_part,) = mode_one_blocks([early], snapshots, mode_one_test, block)
    early_sent = exchange(early_part, "gy", first)
    after_early = lax.optimization_barrier((snapshots, early_part))[0]
    late_part, high, low = mode_one_blocks(
        [late, high_names, low_names], after_early, mode_one_test, block
    )
    late_sent = exchange(late_part, "gy", first)
    high = high + early_sent
    side_input = lax.optimization_barrier((snapshots, high))[0]
    low = low + late_sent
    low = low + exchange(high, "gy", rest[0])
    for bit in rest[1:]:
        keep = [n for n, j in enumerate(low_names) if not j & bit]
        send = [low_names.index(low_names[n] ^ bit) for n in keep]
        moved = exchange(jnp.stack([low[n] for n in send]), "gy", bit)
        low = jnp.stack([low[n] for n in keep]) + moved
        low_names = [low_names[n] for n in keep]
    other = exchange(low, "gy", last)

    sent, kept = core_products(side_input, row_sketch, column_sketch, rank)
    core_shape = (2,) + kept.shape
    value = (kept + exchange(sent, "gx", bits_x[0])).reshape(-1, rank)
    two_input = lax.optimization_barrier((snapshots, kept))[0]
    sent, two = two_products(two_input, mode_two_test)
    for bit in bits_x[1:]:
        keep, send = halves(value, bit, "gx")
        value = keep + exchange(send, "gx", bit)
    two = two + exchange(sent, "gx", bits_x[0])
    for bit in bits_x[1:]:
        two = two + exchange(two, "gx", bit)
    around = [bit for bit in bits_y if bit != scatter_bits[-1]]
    for bit in around[:-2]:
        value = value + exchange(value, "gy", bit)
    core_moved = exchange(value, "gy", around[-2])
    rows_and_core, gram = finish_rows(low_names, low, other, value, core_moved, old_mode_one)
    core_at = len(low_names) * block

    for bit in bits_x:
        gram = gram + exchange(gram, "gx", bit)
    for n, bit in enumerate(scatter_bits):
        gram_moved = exchange(gram, "gy", bit)
        if n < len(scatter_bits) - 1:
            gram = gram + gram_moved

    one, next_one = scatter_bits[-1], scatter_bits[0]
    own = rows_and_core
    by_one = exchange(own, "gy", one)
    by_next = exchange(own[:core_at], "gy", next_one)
    corner_0 = exchange(by_one[:block], "gy", next_one)
    corner_1 = exchange(by_next[block:core_at], "gy", one)
    pieces = [own, by_one, by_next, corner_0, corner_1]
    sizes = [core_at, core_at, core_at, block, block]
    piece_names = list(low_names)
    piece_names += [j ^ one for j in low_names] + [j ^ next_one for j in low_names]
    piece_names += [low_names[0] ^ one ^ next_one, low_names[1] ^ one ^ next_one]
    for bit in scatter_bits[1:-1]:
        pieces = pieces + [exchange(p[:size], "gy", bit) for p, size in zip(pieces, sizes)]
        sizes = sizes + sizes
        piece_names = piece_names + [j ^ bit for j in piece_names]
    value = own[core_at:] + by_one[core_at:]
    value = value + exchange(value, "gy", around[-1])

    first_x = bits_x[0]
    places = [j for j in range(wide) if not j & first_x] + [j for j in range(wide) if j & first_x]
    shares = places[: wide // 2]
    basis_out, *parts = finish(
        piece_names, places, gram, gram_moved, snapshots, pieces, sizes, root_rows
    )
    projected = []
    for t in range(moments):
        sent, passed, kept = parts[3 * t : 3 * t + 3]
        moved = exchange(sent, "gx", first_x)
        kept = kept + moved[0]
        passed = passed + moved[1:]
        held = list(shares)
        for bit in bits_x[1:]:
            keep = [m for m, j in enumerate(held) if not j & bit]
            send = [held.index(held[m] ^ bit) for m in keep]
            send = jnp.stack([passed[m - 1] for m in send]).astype(BF16)
            moved = exchange(send, "gx", bit).astype(F32)
            kept = kept + moved[0]
            if len(keep) > 1:
                passed = jnp.stack([passed[m - 1] for m in keep[1:]]) + moved[1:]
            held = [held[m] for m in keep]
        projected.append(kept)
    projected = jnp.stack(projected, axis=1) / root_rows

    two_back = exchange(two, "gx", first_x)
    mode_two = old_mode_two + joined(two, two_back, first_x, "gx")
    for bit in reversed(bits_x):
        value = joined(value, exchange(value, "gx", bit), bit, "gx")
    stacked = value.reshape(core_shape)
    core = old_core
    for t in range(moments):
        term = jnp.concatenate(list(stacked[t]), axis=1)
        core = core + time_mix[:, t][:, None, None] * term
    return (basis_out, mode_two, projected, core)


def solution(mesh):
    placed = (
        P(None, "gx", "gy"),
        P(None, "gy", None),
        P(None, "gx", None),
        P(None, "gx"),
        P(None, "gy"),
        P("gx", None),
        P("gy", None),
        P(),
        P(),
    )

    return jax.shard_map(
        body,
        mesh=mesh,
        in_specs=placed,
        out_specs=(P(("gx", "gy"), None), P("gy", None), P("gx", None, "gy"), P()),
        check_vma=False,
    )
```

time: 316 us -> 97.1 us (0.31)
  waiting for transfers between devices: 229 us -> 31.7 us
  matrix products: 35.6 us -> 0 us
  Pallas kernels: 0 us -> 33.6 us
  other arithmetic: 31.7 us -> 4.94 us
  starting transfers between devices: 0.34 us -> 23.2 us
  between operations: 13.9 us -> 1.06 us
    psum x3 -> x0, waiting for transfers between devices: 212 us -> none  [the longest x1 117 us: body(): core = old_core + lax.psum(core_part, ('gx', 'gy'))]
    dot_general x7 -> x0, matrix products: 34.7 us -> none  [the longest x1 6.82 us: body(): jnp.einsum('trc,tck->rk', snapshots, mode_one_test, preferred_element_typ...]
    pallas_call x0 -> x6, Pallas kernels: none -> 33.6 us  [the longest x1 10.1 us: finish(): pl.pallas_call(functools.partial(finish_kernel, root_rows, names, places,...]
    ppermute x0 -> x25, waiting for transfers between devices: none -> 31.7 us  [exchange(): return lax.ppermute(value, axis, [(i, i ^ bit) for i in range(size)])]
    ppermute x0 -> x25, starting transfers between devices: none -> 23.2 us  [exchange(): return lax.ppermute(value, axis, [(i, i ^ bit) for i in range(size)])]
    another operation x5 -> x2, other arithmetic: 22.9 us -> 0.04 us  [body(): projected = jnp.stack(projected, axis=1) / root_rows]
    reduce_scatter x1 -> x0, waiting for transfers between devices: 17.5 us -> none  [body(): lax.psum_scatter(projected_part, 'gx', scatter_dimension=0, tiled=True)]
    add x3 -> x13, other arithmetic: 7.05 us -> 3.85 us  [the longest x1 1.78 us: body(): core = core + time_mix[:, t][:, None, None] * term]
  transfers between devices with their start and end apart: 4 -> 25, of which waited for: 4 -> 10; matrix products, arithmetic and copies ran while one was open for 19% -> 3% of each run, Pallas kernels for 0% -> 24%
where the time goes in v1:
time: 97.1 us; the launch traced here: 96.8 us
  Pallas kernels  33.6 us (35%)
  waiting for transfers between devices  31.7 us (33%)
  starting transfers between devices  23.2 us (24%)
  other arithmetic  4.94 us (5%)
  local copies, waits for them, and re-layouts  2.32 us (2%)
  between operations  1.06 us (1%)
    ppermute x25, waiting for transfers between devices, exchange(): return lax.ppermute(value, axis, [(i, i ^ bit) for i in range(size)])  31.7 us
    ppermute x25, starting transfers between devices, exchange(): return lax.ppermute(value, axis, [(i, i ^ bit) for i in range(size)])  23.2 us
    pallas_call x1, Pallas kernels, finish(): pl.pallas_call(functools.partial(finish_kernel, root_rows, names, places,...  10.1 us
    pallas_call x2, Pallas kernels, mode_one_blocks(): pl.pallas_call(functools.partial(mode_one_kernel, groups), in_specs=[HBM,...  9.01 us
    pallas_call x1, Pallas kernels, core_products(): pl.pallas_call(core_kernel, in_specs=[HBM, VMEM, VMEM], out_specs=[VMEM,...  7.45 us
    pallas_call x1, Pallas kernels, two_products(): pl.pallas_call(two_kernel, in_specs=[HBM, VMEM], out_specs=[VMEM, VMEM],...  6.19 us
    unnamed x37, local copies, waits for them, and re-layouts  2.24 us
  transfers between devices with their start and end apart: 25, of which 10 were waited for; matrix products, arithmetic and copies ran while one was open for 3% of the time, Pallas kernels for 24%

profile of v1, /device:TPU:0, one launch (start us, length us, event | category | flops | bytes accessed | tf_op | source)
XLA Modules:
  0.0 96.8 jit_solution(10030906667406918031)
XLA Ops:
  0.6 3.0 %mode_one.2 = f32[2,256,128]{2,1,0:T(8,128)} custom-call(bf16[2,2048,1024]{2,1,0:T(8,128)(2,1)} %snap_hbm.6, bf16[2,1024,128]{2,1,0:T(8,128)(2,1)} %test_hbm.3), custom_call_target="tpu_custom_call" | custom-call | flops 536870912 | bytes 4194304 | tf_op jit(solution)/shard_map/mode_one/pallas_call | solution.py:94
  3.6 3.1 %collective-permute-start.1 = (f32[2,256,128]{2,1,0:T(8,128)}, f32[2,256,128]{2,1,0:T(8,128)S(1)}, u32[]{:S(2)}, u32[]{:S(2)}) collective-permute-start(f32[2,256,128]{2,1,0:T(8,128)} %mode_one.2), channel_id=1, source_target_pairs={{0,1},{1,0},{2,3},{3,2},{4,5},{5,4},{6,7},{7,6},{8,9},{9,8},{10,11... | collective-permute-start | bytes 786440 | tf_op jit(solution)/shard_map/ppermute | solution.py:23
  6.7 6.0 %mode_one.3 = (f32[2,256,128]{2,1,0:T(8,128)}, f32[2,256,128]{2,1,0:T(8,128)}, f32[2,256,128]{2,1,0:T(8,128)}) custom-call(bf16[2,2048,1024]{2,1,0:T(8,128)(2,1)} %snap_hbm.6, bf16[2,1024,128]{2,1,0:T(8,128)(2,1)} %test_hbm.3), custom_call_target="tpu_custom_call" | custom-call | flops 1610612736 | bytes 12582912 | tf_op jit(solution)/shard_map/mode_one/pallas_call | solution.py:94
  13.2 1.0 %add.71 = f32[2,256,128]{2,1,0:T(8,128)S(1)} add(f32[2,256,128]{2,1,0:T(8,128)} %get-tuple-element.26, f32[2,256,128]{2,1,0:T(8,128)S(1)} %collective-permute-done.1) | non-fusion elementwise | flops 65536 | bytes 786432 | tf_op jit(solution)/shard_map/add | solution.py:425
  14.2 7.4 %core_tile.1 = (f32[2,256,128]{2,1,0:T(8,128)}, f32[2,256,128]{2,1,0:T(8,128)}) custom-call(bf16[2,2048,1024]{2,1,0:T(8,128)(2,1)} %snap_hbm.6, bf16[256,2048]{1,0:T(8,128)(2,1)} %row_ref.1, bf16[256,1024]{1,0:T(8,128)(2,1)} %column_ref.1), custom_call_target="tpu_custom_call" | custom-call | flops 4294967296 | bytes 8388608 | tf_op jit(solution)/shard_map/core_tile/pallas_call | solution.py:156
  21.8 1.8 %collective-permute-start = (f32[2,256,128]{2,1,0:T(8,128)S(1)}, f32[2,256,128]{2,1,0:T(8,128)S(1)}, u32[]{:S(2)}, u32[]{:S(2)}) collective-permute-start(f32[2,256,128]{2,1,0:T(8,128)S(1)} %copy-done.17), channel_id=1, source_target_pairs={{0,1},{1,0},{2,3},{3,2},{4,5},{5,4},{6,7},{7,6},{8,9},{9,8},{10,11... | collective-permute-start | bytes 786440 | tf_op jit(solution)/shard_map/ppermute | solution.py:23
  23.6 1.6 %collective-permute-start.2 = (f32[2,256,128]{2,1,0:T(8,128)S(1)}, f32[2,256,128]{2,1,0:T(8,128)S(1)}, u32[]{:S(2)}, u32[]{:S(2)}) collective-permute-start(f32[2,256,128]{2,1,0:T(8,128)S(1)} %add.71), channel_id=1, source_target_pairs={{0,2},{1,3},{2,0},{3,1},{4,6},{5,7},{6,4},{7,5},{8,10},{9,11},{10,... | collective-permute-start | bytes 786440 | tf_op jit(solution)/shard_map/ppermute | solution.py:23
  25.1 6.2 %two_tile.1 = (f32[512,128]{1,0:T(8,128)}, f32[512,128]{1,0:T(8,128)}) custom-call(bf16[2,2048,1024]{2,1,0:T(8,128)(2,1)} %snap_hbm.6, bf16[2,2048,128]{2,1,0:T(8,128)(2,1)} %test_ref.1), custom_call_target="tpu_custom_call" | custom-call | flops 2147483648 | bytes 8388608 | tf_op jit(solution)/shard_map/two_tile/pallas_call | solution.py:201
  31.5 1.6 %collective-permute-start.5 = (f32[256,128]{1,0:T(8,128)S(1)}, f32[256,128]{1,0:T(8,128)S(1)}, u32[]{:S(2)}, u32[]{:S(2)}) collective-permute-start(f32[256,128]{1,0:T(8,128)S(1)} %constant_dynamic-slice_fusion), channel_id=1, source_target_pairs={{0,16},{8,24},{16,0},{24,8},{1,17},{9,25},{17,1},{25,9},{2,18},{10... | collective-permute-start | bytes 393224 | tf_op jit(solution)/shard_map/ppermute | solution.py:23
  33.1 2.7 %collective-permute-start.3 = (f32[2,256,128]{2,1,0:T(8,128)S(1)}, f32[2,256,128]{2,1,0:T(8,128)S(1)}, u32[]{:S(2)}, u32[]{:S(2)}) collective-permute-start(f32[2,256,128]{2,1,0:T(8,128)S(1)} %add_add_fusion.mine_ref), channel_id=1, source_target_pairs={{0,4},{1,5},{2,6},{3,7},{4,0},{5,1},{6,2},{7,3},{8,12},{9,13},{10,... | collective-permute-start | bytes 786440 | tf_op jit(solution)/shard_map/ppermute | solution.py:23
  35.8 1.7 %collective-permute-done.5 = f32[256,128]{1,0:T(8,128)S(1)} collective-permute-done((f32[256,128]{1,0:T(8,128)S(1)}, f32[256,128]{1,0:T(8,128)S(1)}, u32[]{:S(2)}, u32[]{:S(2)}) %collective-permute-start.5) | collective-permute-done | bytes 131104 | tf_op jit(solution)/shard_map/ppermute | solution.py:23
  38.1 9.9 %collective-permute-done.3.other_ref = f32[2,256,128]{2,1,0:T(8,128)S(1)} collective-permute-done((f32[2,256,128]{2,1,0:T(8,128)S(1)}, f32[2,256,128]{2,1,0:T(8,128)S(1)}, u32[]{:S(2)}, u32[]{:S(2)}) %collective-permute-start.3) | collective-permute-done | bytes 262176 | tf_op jit(solution)/shard_map/ppermute | solution.py:23
  50.3 1.3 %collective-permute-done.7 = f32[128,128]{1,0:T(8,128)S(1)} collective-permute-done((f32[128,128]{1,0:T(8,128)S(1)}, f32[128,128]{1,0:T(8,128)S(1)}, u32[]{:S(2)}, u32[]{:S(2)}) %collective-permute-start.7) | collective-permute-done | bytes 65568 | tf_op jit(solution)/shard_map/ppermute | solution.py:23
  51.5 1.5 %collective-permute-start.8 = (f32[128,128]{1,0:T(8,128)S(1)}, f32[128,128]{1,0:T(8,128)S(1)}, u32[]{:S(2)}, u32[]{:S(2)}) collective-permute-start(f32[128,128]{1,0:T(8,128)S(1)} %add.77), channel_id=1, source_target_pairs={{0,16},{8,24},{16,0},{24,8},{1,17},{9,25},{17,1},{25,9},{2,18},{10... | collective-permute-start | bytes 196616 | tf_op jit(solution)/shard_map/ppermute | solution.py:23
  53.0 5.7 %collective-permute-done.8 = f32[128,128]{1,0:T(8,128)S(1)} collective-permute-done((f32[128,128]{1,0:T(8,128)S(1)}, f32[128,128]{1,0:T(8,128)S(1)}, u32[]{:S(2)}, u32[]{:S(2)}) %collective-permute-start.8) | collective-permute-done | bytes 65568 | tf_op jit(solution)/shard_map/ppermute | solution.py:23
  59.4 3.6 %collective-permute-done.9 = f32[128,128]{1,0:T(8,128)S(1)} collective-permute-done((f32[128,128]{1,0:T(8,128)S(1)}, f32[128,128]{1,0:T(8,128)S(1)}, u32[]{:S(2)}, u32[]{:S(2)}) %collective-permute-start.9) | collective-permute-done | bytes 65568 | tf_op jit(solution)/shard_map/ppermute | solution.py:23
  63.1 1.8 %collective-permute-start.10 = (f32[128,128]{1,0:T(8,128)S(1)}, f32[128,128]{1,0:T(8,128)S(1)}, u32[]{:S(2)}, u32[]{:S(2)}) collective-permute-start(f32[128,128]{1,0:T(8,128)S(1)} %add.79.gram_ref), channel_id=1, source_target_pairs={{0,2},{1,3},{2,0},{3,1},{4,6},{5,7},{6,4},{7,5},{8,10},{9,11},{10,... | collective-permute-start | bytes 196616 | tf_op jit(solution)/shard_map/ppermute | solution.py:23
  65.9 2.1 %collective-permute-start.22 = (f32[256,128]{1,0:T(8,128)S(1)}, f32[256,128]{1,0:T(8,128)S(1)}, u32[]{:S(2)}, u32[]{:S(2)}) collective-permute-start(f32[256,128]{1,0:T(8,128)S(1)} %get-tuple-element.50), channel_id=1, source_target_pairs={{0,4},{1,5},{2,6},{3,7},{4,0},{5,1},{6,2},{7,3},{8,12},{9,13},{10,... | collective-permute-start | bytes 393224 | tf_op jit(solution)/shard_map/ppermute | solution.py:23
  68.0 5.1 %collective-permute-done.22 = f32[256,128]{1,0:T(8,128)S(1)} collective-permute-done((f32[256,128]{1,0:T(8,128)S(1)}, f32[256,128]{1,0:T(8,128)S(1)}, u32[]{:S(2)}, u32[]{:S(2)}) %collective-permute-start.22) | collective-permute-done | bytes 131104 | tf_op jit(solution)/shard_map/ppermute | solution.py:23
  75.2 10.1 %finish.1 = (f32[256,128]{1,0:T(8,128)}, f32[2,32,1024]{2,1,0:T(8,128)}, f32[1,32,1024]{2,1,0:T(8,128)}, f32[32,1024]{1,0:T(8,128)}, f32[2,32,1024]{2,1,0:T(8,12...) custom-call(f32[128,128]{1,0:T(8,128)} %copy-done.6, f32[128,128]{1,0:T(8,128)} %copy-done.15, ...), custom_call_target="tpu_custom_call" | custom-call | flops 2147483648 | bytes 8388608 | tf_op jit(solution)/shard_map/finish/pallas_call | solution.py:371
  88.1 1.5 %collective-permute-start.19 = (bf16[1,32,1024]{2,1,0:T(8,128)(2,1)S(1)}, bf16[1,32,1024]{2,1,0:T(8,128)(2,1)S(1)}, u32[]{:S(2)}, u32[]{:S(2)}) collective-permute-start(bf16[1,32,1024]{2,1,0:T(8,128)(2,1)S(1)} %fusion.5), channel_id=1, source_target_pairs={{0,16},{8,24},{16,0},{24,8},{1,17},{9,25},{17,1},{25,9},{2,18},{10... | collective-permute-start | bytes 196616 | tf_op jit(solution)/shard_map/ppermute | solution.py:23
  90.3 2.4 %collective-permute-done.19 = bf16[1,32,1024]{2,1,0:T(8,128)(2,1)S(1)} collective-permute-done((bf16[1,32,1024]{2,1,0:T(8,128)(2,1)S(1)}, bf16[1,32,1024]{2,1,0:T(8,128)(2,1)S(1)}, u32[]{:S(2)}, u32[]{:S(2)}) %collective-permute-start.19) | collective-permute-done | bytes 65568 | tf_op jit(solution)/shard_map/ppermute | solution.py:23
  92.7 1.2 %collective-permute-done.21 = bf16[1,32,1024]{2,1,0:T(8,128)(2,1)S(1)} collective-permute-done((bf16[1,32,1024]{2,1,0:T(8,128)(2,1)S(1)}, bf16[1,32,1024]{2,1,0:T(8,128)(2,1)S(1)}, u32[]{:S(2)}, u32[]{:S(2)}) %collective-permute-start.21) | collective-permute-done | bytes 65568 | tf_op jit(solution)/shard_map/ppermute | solution.py:23
  95.0 1.8 %multiply_add_fusion = f32[9,256,256]{2,1,0:T(8,128)} fusion(f32[9,256,256]{2,1,0:T(8,128)S(1)} %copy-done.2, f32[256,256]{1,0:T(8,128)S(1)} %get-tuple-element.55, f32[9]{0:T(128)S(1)} %get-tuple-element.53, f32[256,256]{1,0:T(8,128)S(1)} %get-tuple-element.54, f32[9]{0:T(128)S(1)} %get-tuple-element.52), kind=kLoop, calls=%fused_computation | loop fusion | flops 2359296 | bytes 5242952 | tf_op jit(solution)/shard_map/add | solution.py:513
  (95 shorter events, 11.7 us)
Async XLA Ops:
  3.6 9.6 %collective-permute-start.1 = (f32[2,256,128]{2,1,0:T(8,128)}, f32[2,256,128]{2,1,0:T(8,128)S(1)}, u32[]{:S(2)}, u32[]{:S(2)}) collective-permute-start(f32[2,256,128]{2,1,0:T(8,128)} %mode_one.2), channel_id=1, source_target_pairs={{0,1},{1,0},{2,3},{3,2},{4,5},{5,4},{6,7},{7,6},{8,9},{9,8},{10,11... | collective-permute-start | bytes 786440 | tf_op jit(solution)/shard_map/ppermute | solution.py:23
  21.7 9.8 %collective-permute-start.4 = (f32[2,256,128]{2,1,0:T(8,128)}, f32[2,256,128]{2,1,0:T(8,128)S(1)}, u32[]{:S(2)}, u32[]{:S(2)}) collective-permute-start(f32[2,256,128]{2,1,0:T(8,128)} %get-tuple-element.29), channel_id=1, source_target_pairs={{0,8},{8,0},{16,24},{24,16},{1,9},{9,1},{17,25},{25,17},{2,10},{10... | collective-permute-start | bytes 786440 | tf_op jit(solution)/shard_map/ppermute | solution.py:23
  21.8 11.3 %collective-permute-start = (f32[2,256,128]{2,1,0:T(8,128)S(1)}, f32[2,256,128]{2,1,0:T(8,128)S(1)}, u32[]{:S(2)}, u32[]{:S(2)}) collective-permute-start(f32[2,256,128]{2,1,0:T(8,128)S(1)} %copy-done.17), channel_id=1, source_target_pairs={{0,1},{1,0},{2,3},{3,2},{4,5},{5,4},{6,7},{7,6},{8,9},{9,8},{10,11... | collective-permute-start | bytes 786440 | tf_op jit(solution)/shard_map/ppermute | solution.py:23
  23.6 9.5 %collective-permute-start.2 = (f32[2,256,128]{2,1,0:T(8,128)S(1)}, f32[2,256,128]{2,1,0:T(8,128)S(1)}, u32[]{:S(2)}, u32[]{:S(2)}) collective-permute-start(f32[2,256,128]{2,1,0:T(8,128)S(1)} %add.71), channel_id=1, source_target_pairs={{0,2},{1,3},{2,0},{3,1},{4,6},{5,7},{6,4},{7,5},{8,10},{9,11},{10,... | collective-permute-start | bytes 786440 | tf_op jit(solution)/shard_map/ppermute | solution.py:23
  31.4 17.6 %collective-permute-start.15 = (f32[512,128]{1,0:T(8,128)}, f32[512,128]{1,0:T(8,128)S(1)}, u32[]{:S(2)}, u32[]{:S(2)}) collective-permute-start(f32[512,128]{1,0:T(8,128)} %get-tuple-element.35), channel_id=1, source_target_pairs={{0,8},{8,0},{16,24},{24,16},{1,9},{9,1},{17,25},{25,17},{2,10},{10... | collective-permute-start | bytes 786440 | tf_op jit(solution)/shard_map/ppermute | solution.py:23
  31.5 5.9 %collective-permute-start.5 = (f32[256,128]{1,0:T(8,128)S(1)}, f32[256,128]{1,0:T(8,128)S(1)}, u32[]{:S(2)}, u32[]{:S(2)}) collective-permute-start(f32[256,128]{1,0:T(8,128)S(1)} %constant_dynamic-slice_fusion), channel_id=1, source_target_pairs={{0,16},{8,24},{16,0},{24,8},{1,17},{9,25},{17,1},{25,9},{2,18},{10... | collective-permute-start | bytes 393224 | tf_op jit(solution)/shard_map/ppermute | solution.py:23
  33.1 14.9 %collective-permute-start.3 = (f32[2,256,128]{2,1,0:T(8,128)S(1)}, f32[2,256,128]{2,1,0:T(8,128)S(1)}, u32[]{:S(2)}, u32[]{:S(2)}) collective-permute-start(f32[2,256,128]{2,1,0:T(8,128)S(1)} %add_add_fusion.mine_ref), channel_id=1, source_target_pairs={{0,4},{1,5},{2,6},{3,7},{4,0},{5,1},{6,2},{7,3},{8,12},{9,13},{10,... | collective-permute-start | bytes 786440 | tf_op jit(solution)/shard_map/ppermute | solution.py:23
  37.5 10.5 %collective-permute-start.6 = (f32[256,128]{1,0:T(8,128)S(1)}, f32[256,128]{1,0:T(8,128)S(1)}, u32[]{:S(2)}, u32[]{:S(2)}) collective-permute-start(f32[256,128]{1,0:T(8,128)S(1)} %dynamic-slice_add_fusion.core_ref), channel_id=1, source_target_pairs={{0,1},{1,0},{2,3},{3,2},{4,5},{5,4},{6,7},{7,6},{8,9},{9,8},{10,11... | collective-permute-start | bytes 393224 | tf_op jit(solution)/shard_map/ppermute | solution.py:23
  48.9 16.4 %collective-permute-start.11 = (f32[768,128]{1,0:T(8,128)S(1)}, f32[768,128]{1,0:T(8,128)S(1)}, u32[]{:S(2)}, u32[]{:S(2)}) collective-permute-start(f32[768,128]{1,0:T(8,128)S(1)} %get-tuple-element.31.refs_0_), channel_id=1, source_target_pairs={{0,2},{1,3},{2,0},{3,1},{4,6},{5,7},{6,4},{7,5},{8,10},{9,11},{10,... | collective-permute-start | bytes 1179656 | tf_op jit(solution)/shard_map/ppermute | solution.py:23
  49.0 10.3 %collective-permute-start.16 = (f32[512,128]{1,0:T(8,128)S(1)}, f32[512,128]{1,0:T(8,128)S(1)}, u32[]{:S(2)}, u32[]{:S(2)}) collective-permute-start(f32[512,128]{1,0:T(8,128)S(1)} %add.80), channel_id=1, source_target_pairs={{0,16},{8,24},{16,0},{24,8},{1,17},{9,25},{17,1},{25,9},{2,18},{10... | collective-permute-start | bytes 786440 | tf_op jit(solution)/shard_map/ppermute | solution.py:23
  49.6 15.3 %collective-permute-start.12 = (f32[512,128]{1,0:T(8,128)S(1)}, f32[512,128]{1,0:T(8,128)S(1)}, u32[]{:S(2)}, u32[]{:S(2)}) collective-permute-start(f32[512,128]{1,0:T(8,128)S(1)} %slice.45), channel_id=1, source_target_pairs={{0,1},{1,0},{2,3},{3,2},{4,5},{5,4},{6,7},{7,6},{8,9},{9,8},{10,11... | collective-permute-start | bytes 786440 | tf_op jit(solution)/shard_map/ppermute | solution.py:23
  51.5 7.2 %collective-permute-start.8 = (f32[128,128]{1,0:T(8,128)S(1)}, f32[128,128]{1,0:T(8,128)S(1)}, u32[]{:S(2)}, u32[]{:S(2)}) collective-permute-start(f32[128,128]{1,0:T(8,128)S(1)} %add.77), channel_id=1, source_target_pairs={{0,16},{8,24},{16,0},{24,8},{1,17},{9,25},{17,1},{25,9},{2,18},{10... | collective-permute-start | bytes 196616 | tf_op jit(solution)/shard_map/ppermute | solution.py:23
  58.7 4.3 %collective-permute-start.9 = (f32[128,128]{1,0:T(8,128)S(1)}, f32[128,128]{1,0:T(8,128)S(1)}, u32[]{:S(2)}, u32[]{:S(2)}) collective-permute-start(f32[128,128]{1,0:T(8,128)S(1)} %add.78), channel_id=1, source_target_pairs={{0,1},{1,0},{2,3},{3,2},{4,5},{5,4},{6,7},{7,6},{8,9},{9,8},{10,11... | collective-permute-start | bytes 196616 | tf_op jit(solution)/shard_map/ppermute | solution.py:23
  59.3 26.1 %collective-permute-start.17 = (f32[512,128]{1,0:T(8,128)S(1)}, f32[512,128]{1,0:T(8,128)S(1)}, u32[]{:S(2)}, u32[]{:S(2)}) collective-permute-start(f32[512,128]{1,0:T(8,128)S(1)} %add.81), channel_id=1, source_target_pairs={{0,8},{8,0},{16,24},{24,16},{1,9},{9,1},{17,25},{25,17},{2,10},{10... | collective-permute-start | bytes 786440 | tf_op jit(solution)/shard_map/ppermute | solution.py:23
  63.1 10.8 %collective-permute-start.10 = (f32[128,128]{1,0:T(8,128)S(1)}, f32[128,128]{1,0:T(8,128)S(1)}, u32[]{:S(2)}, u32[]{:S(2)}) collective-permute-start(f32[128,128]{1,0:T(8,128)S(1)} %add.79.gram_ref), channel_id=1, source_target_pairs={{0,2},{1,3},{2,0},{3,1},{4,6},{5,7},{6,4},{7,5},{8,10},{9,11},{10,... | collective-permute-start | bytes 196616 | tf_op jit(solution)/shard_map/ppermute | solution.py:23
  64.9 9.0 %collective-permute-start.14 = (f32[256,128]{1,0:T(8,128)S(1)}, f32[256,128]{1,0:T(8,128)S(1)}, u32[]{:S(2)}, u32[]{:S(2)}) collective-permute-start(f32[256,128]{1,0:T(8,128)S(1)} %slice.57), channel_id=1, source_target_pairs={{0,2},{1,3},{2,0},{3,1},{4,6},{5,7},{6,4},{7,5},{8,10},{9,11},{10,... | collective-permute-start | bytes 393224 | tf_op jit(solution)/shard_map/ppermute | solution.py:23
  65.3 8.6 %collective-permute-start.13 = (f32[256,128]{1,0:T(8,128)S(1)}, f32[256,128]{1,0:T(8,128)S(1)}, u32[]{:S(2)}, u32[]{:S(2)}) collective-permute-start(f32[256,128]{1,0:T(8,128)S(1)} %get-tuple-element.51), channel_id=1, source_target_pairs={{0,1},{1,0},{2,3},{3,2},{4,5},{5,4},{6,7},{7,6},{8,9},{9,8},{10,11... | collective-permute-start | bytes 393224 | tf_op jit(solution)/shard_map/ppermute | solution.py:23
  65.9 7.3 %collective-permute-start.22 = (f32[256,128]{1,0:T(8,128)S(1)}, f32[256,128]{1,0:T(8,128)S(1)}, u32[]{:S(2)}, u32[]{:S(2)}) collective-permute-start(f32[256,128]{1,0:T(8,128)S(1)} %get-tuple-element.50), channel_id=1, source_target_pairs={{0,4},{1,5},{2,6},{3,7},{4,0},{5,1},{6,2},{7,3},{8,12},{9,13},{10,... | collective-permute-start | bytes 393224 | tf_op jit(solution)/shard_map/ppermute | solution.py:23
  73.2 13.6 %collective-permute-start.23 = (f32[256,128]{1,0:T(8,128)S(1)}, f32[256,128]{1,0:T(8,128)S(1)}, u32[]{:S(2)}, u32[]{:S(2)}) collective-permute-start(f32[256,128]{1,0:T(8,128)S(1)} %add.90), channel_id=1, source_target_pairs={{0,16},{8,24},{16,0},{24,8},{1,17},{9,25},{17,1},{25,9},{2,18},{10... | collective-permute-start | bytes 393224 | tf_op jit(solution)/shard_map/ppermute | solution.py:23
  85.4 1.8 %collective-permute-start.18 = (f32[2,32,1024]{2,1,0:T(8,128)}, f32[2,32,1024]{2,1,0:T(8,128)S(1)}, u32[]{:S(2)}, u32[]{:S(2)}) collective-permute-start(f32[2,32,1024]{2,1,0:T(8,128)} %get-tuple-element.37), channel_id=1, source_target_pairs={{0,8},{8,0},{16,24},{24,16},{1,9},{9,1},{17,25},{25,17},{2,10},{10... | collective-permute-start | bytes 786440 | tf_op jit(solution)/shard_map/ppermute | solution.py:23
  86.3 3.2 %collective-permute-start.20 = (f32[2,32,1024]{2,1,0:T(8,128)}, f32[2,32,1024]{2,1,0:T(8,128)S(1)}, u32[]{:S(2)}, u32[]{:S(2)}) collective-permute-start(f32[2,32,1024]{2,1,0:T(8,128)} %get-tuple-element.40), channel_id=1, source_target_pairs={{0,8},{8,0},{16,24},{24,16},{1,9},{9,1},{17,25},{25,17},{2,10},{10... | collective-permute-start | bytes 786440 | tf_op jit(solution)/shard_map/ppermute | solution.py:23
  86.8 8.0 %collective-permute-start.24 = (f32[512,128]{1,0:T(8,128)S(1)}, f32[512,128]{1,0:T(8,128)S(1)}, u32[]{:S(2)}, u32[]{:S(2)}) collective-permute-start(f32[512,128]{1,0:T(8,128)S(1)} %maximum_select_fusion.2), channel_id=1, source_target_pairs={{0,8},{8,0},{16,24},{24,16},{1,9},{9,1},{17,25},{25,17},{2,10},{10... | collective-permute-start | bytes 786440 | tf_op jit(solution)/shard_map/ppermute | solution.py:23
  88.1 4.5 %collective-permute-start.19 = (bf16[1,32,1024]{2,1,0:T(8,128)(2,1)S(1)}, bf16[1,32,1024]{2,1,0:T(8,128)(2,1)S(1)}, u32[]{:S(2)}, u32[]{:S(2)}) collective-permute-start(bf16[1,32,1024]{2,1,0:T(8,128)(2,1)S(1)} %fusion.5), channel_id=1, source_target_pairs={{0,16},{8,24},{16,0},{24,8},{1,17},{9,25},{17,1},{25,9},{2,18},{10... | collective-permute-start | bytes 196616 | tf_op jit(solution)/shard_map/ppermute | solution.py:23
  89.6 4.3 %collective-permute-start.21 = (bf16[1,32,1024]{2,1,0:T(8,128)(2,1)S(1)}, bf16[1,32,1024]{2,1,0:T(8,128)(2,1)S(1)}, u32[]{:S(2)}, u32[]{:S(2)}) collective-permute-start(bf16[1,32,1024]{2,1,0:T(8,128)(2,1)S(1)} %fusion.1), channel_id=1, source_target_pairs={{0,16},{8,24},{16,0},{24,8},{1,17},{9,25},{17,1},{25,9},{2,18},{10... | collective-permute-start | bytes 196616 | tf_op jit(solution)/shard_map/ppermute | solution.py:23
  (19 other events, 178.1 us)
